TPU v7x, 128 devices: a whole 4x4x4 slice. The times are simulated.
128 devices in a mesh: section: 2 (over core), dp: 16 (over y, x), mp: 4 (over z).
Axes of the slice: x: 4, y: 4, z: 4, core: 2. Of those that a mesh axis runs over, the one named last changes fastest.
Arguments:
- out_grad: bfloat16 [512, 8192], P('dp', 'mp'), may hold values from -6 to 6
- upper_w: bfloat16 [2, 14336, 8192], P('section', 'dp', 'mp'), may hold values from -0.0625 to 0.0625
- lower_w: bfloat16 [2, 8192, 14336], P('section', 'mp', 'dp'), may hold values from -0.046875 to 0.046875
- upper_in: bfloat16 [2, 512, 14336], P('section', None, 'mp'), may hold values from -6 to 6
- lower_in: bfloat16 [2, 512, 8192], P('section', None, 'dp'), may hold values from -6 to 6
- upper_deriv: bfloat16 [2, 512, 14336], P('section', 'mp', 'dp'), may hold values from 0.3984375 to 1.5
- lower_deriv: bfloat16 [2, 512, 8192], P('section', 'dp', 'mp'), may hold values from 0.3984375 to 1.5
- proj_upper_in: bfloat16 [2, 64, 14336], P('section', None, 'mp'), may hold values from -0.046875 to 0.046875
- proj_upper_out: bfloat16 [2, 64, 8192], P('section', None, 'mp'), may hold values from -0.0625 to 0.0625
- proj_lower_in: bfloat16 [2, 64, 8192], P('section', None, 'dp'), may hold values from -0.0625 to 0.0625
- proj_lower_out: bfloat16 [2, 64, 14336], P('section', None, 'dp'), may hold values from -0.046875 to 0.046875
- window_ids: int32 [512], replicated, may hold values from 0 to 255
- window_slot: int32 [256], replicated, may hold values from 0 to 255, each once
Outputs:
- section_grads: bfloat16 [2, 512, 8192], P('section', 'dp', 'mp')
- sketches: float32 [2, 2, 256, 4096], P('section', None, ('dp', 'mp'))
Inputs may be any that keep to these rules, and one draw needn't show every extreme that they name: Each window has exactly one row: window_slot is a permutation.
All inputs are finite; a program needn't handle non-finite values.
Results may differ from a plain program's by a relative error of at most 0.0075.
Values may be sent and summed in bfloat16 or wider, within the bound.
No kernel may reach another device: no remote copies, remote signals or barrier semaphores. Data moves between devices by JAX's collectives and lax.ppermute only.
A program may use at most 128 MiB of HBM per device.

v0:
```python
import jax
import jax.numpy as jnp
from jax import lax
from jax.sharding import PartitionSpec as P


def from_behind(block, axis, distance):
    devices = range(lax.axis_size(axis))
    route = [(i - distance, i) for i in devices if i - distance in devices]
    return lax.ppermute(block, axis, route)


def times_t(left, right):
    return lax.dot_general(
        left, right, (((1,), (1,)), ((), ())), preferred_element_type=jnp.float32
    )


def token_lower(dp_src, mp_src, block_id, inner, tokens_dev, rows_block, quota):
    return dp_src * tokens_dev + block_id * rows_block + mp_src * quota + inner


def token_upper(dp_src, mp_src, block_id, inner, tokens_dev, rows_block, quota, ratio):
    flat_row = dp_src * quota + inner
    return (
        (mp_src * ratio + flat_row // rows_block) * tokens_dev
        + block_id * rows_block
        + flat_row % rows_block
    )


def slots_of(token_rows, window_ids, window_slot):
    total_tokens = window_ids.shape[0]
    picked = token_rows[:, None] == jnp.arange(total_tokens, dtype=jnp.int32)[None, :]
    window_row = jnp.sum(jnp.where(picked, window_ids[None, :], 0), axis=1)
    window_count = window_slot.shape[0]
    matched = window_row[:, None] == jnp.arange(window_count, dtype=jnp.int32)[None, :]
    return jnp.sum(jnp.where(matched, window_slot[None, :], 0), axis=1)


def outer_rows(factors, rank_size):
    left = factors[:, :rank_size]
    right = factors[:, rank_size:]
    return (left[:, :, None] * right[:, None, :]).reshape(factors.shape[0], rank_size * rank_size)


def window_sums(targets, factors, window_count, rank_size):
    matched = (targets[:, None] == jnp.arange(window_count, dtype=jnp.int32)[None, :]).astype(
        jnp.float32
    )
    return lax.dot_general(
        matched,
        outer_rows(factors, rank_size),
        (((0,), (0,)), ((), ())),
        precision=lax.Precision.HIGHEST,
        preferred_element_type=jnp.float32,
    )


def body(
    out_grad,
    upper_w,
    lower_w,
    upper_in,
    lower_in,
    upper_deriv,
    lower_deriv,
    proj_upper_in,
    proj_upper_out,
    proj_lower_in,
    proj_lower_out,
    window_ids,
    window_slot,
):
    section_count = lax.axis_size("section")
    dp_count = lax.axis_size("dp")
    mp_count = lax.axis_size("mp")
    section_index = lax.axis_index("section")
    dp_index = lax.axis_index("dp")
    mp_index = lax.axis_index("mp")
    tokens_dev = out_grad.shape[0]
    width_mp = out_grad.shape[1]
    width_ff = upper_deriv.shape[2]
    width_hidden = upper_in.shape[2]
    width_low = lower_in.shape[2]
    rank_size = proj_upper_in.shape[1]
    ratio = dp_count // mp_count
    block_count = 4
    rows_block = tokens_dev // block_count
    quota = rows_block // mp_count
    weight_up = upper_w[0]
    weight_low = lower_w[0]
    acts_upper = upper_in[0].reshape(dp_count, tokens_dev, width_hidden)
    acts_lower = lower_in[0].reshape(dp_count, tokens_dev, width_low)
    deriv_up = upper_deriv[0].reshape(ratio, tokens_dev, width_ff)
    deriv_low = lower_deriv[0]
    pin_up = proj_upper_in[0]
    pout_up = proj_upper_out[0]
    pin_low = proj_lower_in[0]
    pout_low = proj_lower_out[0]

    def advance(turn, carry):
        received, grads, factors_low, factors_up = carry
        block_id = turn - (section_count - 1 - section_index)
        is_live = (block_id >= 0) & (block_id < block_count)
        block_safe = jnp.clip(block_id, 0, block_count - 1)
        first_row = block_safe * rows_block
        top_block = lax.dynamic_slice_in_dim(out_grad, first_row, rows_block, 0)
        grad_up = jnp.where(section_index == section_count - 1, top_block, received)
        gathered_up = lax.all_gather(grad_up, "dp", axis=0, tiled=True)
        inputs_up = lax.dynamic_slice_in_dim(acts_upper, first_row, rows_block, 1).reshape(
            dp_count * rows_block, width_hidden
        )
        grad_rows = gathered_up
        input_rows = inputs_up
        summed_up = lax.psum_scatter(
            jnp.concatenate(
                [
                    times_t(grad_rows, weight_up),
                    times_t(input_rows, pin_up),
                    times_t(grad_rows, pout_up),
                ],
                axis=1,
            ),
            "mp",
            scatter_dimension=0,
            tiled=True,
        )
        scale_up = lax.dynamic_slice_in_dim(deriv_up, first_row, rows_block, 1).reshape(
            ratio * rows_block, width_ff
        )
        grad_mid = (summed_up[:, :width_ff] * scale_up.astype(jnp.float32)).astype(jnp.bfloat16)
        owned_up = lax.dynamic_slice_in_dim(summed_up[:, width_ff:], dp_index * quota, quota, 0)
        gathered_low = lax.all_gather(grad_mid, "mp", axis=0, tiled=True)
        inputs_low = lax.dynamic_slice_in_dim(acts_lower, first_row, rows_block, 1).reshape(
            dp_count * rows_block, width_low
        )
        grad_rows = gathered_low
        input_rows = inputs_low
        summed_low = lax.psum_scatter(
            jnp.concatenate(
                [
                    times_t(grad_rows, weight_low),
                    times_t(input_rows, pin_low),
                    times_t(grad_rows, pout_low),
                ],
                axis=1,
            ),
            "dp",
            scatter_dimension=0,
            tiled=True,
        )
        scale_low = lax.dynamic_slice_in_dim(deriv_low, first_row, rows_block, 0)
        grad_out = (summed_low[:, :width_mp] * scale_low.astype(jnp.float32)).astype(jnp.bfloat16)
        owned_low = lax.dynamic_slice_in_dim(summed_low[:, width_mp:], mp_index * quota, quota, 0)
        previous = lax.dynamic_slice_in_dim(grads, first_row, rows_block, 0)
        grads = lax.dynamic_update_slice_in_dim(
            grads, jnp.where(is_live, grad_out, previous), first_row, 0
        )
        prev_low = lax.dynamic_slice_in_dim(factors_low, block_safe, 1, 0)
        factors_low = lax.dynamic_update_slice_in_dim(
            factors_low, jnp.where(is_live, owned_low[None], prev_low), block_safe, 0
        )
        prev_up = lax.dynamic_slice_in_dim(factors_up, block_safe, 1, 0)
        factors_up = lax.dynamic_update_slice_in_dim(
            factors_up, jnp.where(is_live, owned_up[None], prev_up), block_safe, 0
        )
        received = from_behind(grad_out, "section", -1)
        return (received, grads, factors_low, factors_up)

    start_carry = (
        jnp.zeros((rows_block, width_mp), jnp.bfloat16),
        jnp.zeros((tokens_dev, width_mp), jnp.bfloat16),
        jnp.zeros((block_count, quota, 2 * rank_size), jnp.float32),
        jnp.zeros((block_count, quota, 2 * rank_size), jnp.float32),
    )
    _, grads, factors_low, factors_up = lax.fori_loop(
        0, block_count + section_count - 1, advance, start_carry
    )
    flat_low = factors_low.reshape(block_count * quota, 2 * rank_size)
    flat_up = factors_up.reshape(block_count * quota, 2 * rank_size)
    window_count = window_slot.shape[0]
    block_grid = jnp.arange(block_count, dtype=jnp.int32)[:, None]
    inner_grid = jnp.arange(quota, dtype=jnp.int32)[None, :]
    tokens_low = token_lower(
        dp_index, mp_index, block_grid, inner_grid, tokens_dev, rows_block, quota
    ).reshape(-1)
    tokens_up = token_upper(
        dp_index, mp_index, block_grid, inner_grid, tokens_dev, rows_block, quota, ratio
    ).reshape(-1)
    low_part = window_sums(
        slots_of(tokens_low, window_ids, window_slot), flat_low, window_count, rank_size
    )
    up_part = window_sums(
        slots_of(tokens_up, window_ids, window_slot), flat_up, window_count, rank_size
    )
    sketch = lax.psum_scatter(
        jnp.stack([low_part, up_part]), ("dp", "mp"), scatter_dimension=1, tiled=True
    )
    return (grads[None], sketch[None])


def solution(mesh):
    placed = (
        P("dp", "mp"),
        P("section", "dp", "mp"),
        P("section", "mp", "dp"),
        P("section", None, "mp"),
        P("section", None, "dp"),
        P("section", "mp", "dp"),
        P("section", "dp", "mp"),
        P("section", None, "mp"),
        P("section", None, "mp"),
        P("section", None, "dp"),
        P("section", None, "dp"),
        P(),
        P(),
    )
    return jax.shard_map(
        body,
        mesh=mesh,
        in_specs=placed,
        out_specs=(P("section", "dp", "mp"), P("section", None, ("dp", "mp"), None)),
        check_vma=False,
    )
```

profile of v0, /device:TPU:0, one launch (start us, length us, event | category | flops | bytes accessed | tf_op | source)
XLA Modules:
  0.0 996.2 jit_solution(14661798061254032778)
XLA Ops:
  8.1 801.4 %while.21 = (s32[]{:T(128)}, bf16[8,2048]{1,0:T(8,128)(2,1)S(1)}, bf16[32,2048]{1,0:T(8,128)(2,1)S(1)}, f32[4,2,128]{2,1,0:T(2,128)S(1)}, f32[4,2,128]{2,1,0:T(2...) while((s32[]{:T(128)}, bf16[8,2048]{1,0:T(8,128)(2,1)S(1)}, ...), condition=%wide.region_3.4_spmd, body=%wide.region_0.3_spmd.sunk | while | flops 1055576576 | bytes 28484304 | solution.py:177
  9.0 24.3 %all_gather.20 = bf16[128,2048]{1,0:T(8,128)(2,1)S(1)} all-gather(bf16[8,2048]{1,0:T(8,128)(2,1)S(1)} %dynamic-slice_select_fusion.2), channel_id=1, replica_groups=mesh['section'=2,'dp'=16,'mp'=4] {'dp'}, dimensions={0}, use_global_device_ids=true | all-gather | bytes 557056 | tf_op jit(solution)/shard_map/while/body/eval_jaxpr/all_gather | solution.py:110
  33.4 1.2 fusion.66
  34.6 3.4 fusion.68
  38.0 1.6 fusion.67
  40.5 1.1 fusion.71
  41.6 20.9 %reduce-scatter.3.cloned.1.call-done = f32[32,1024]{1,0:T(8,128)} async-done(((f32[128,1024]{1,0:T(8,128)}), f32[32,1024]{1,0:T(8,128)}) %reduce-scatter.3.cloned.1.call-update) | async-done | bytes 131088 | tf_op jit(solution)/shard_map/while/body/eval_jaxpr/reduce_scatter | solution.py:116
  63.5 12.2 %all_gather.21 = bf16[128,896]{1,0:T(8,128)(2,1)S(1)} all-gather(bf16[32,896]{1,0:T(8,128)(2,1)S(1)} %fusion.69), channel_id=1, replica_groups=mesh['section'=2,'dp'=16,'mp'=4] {'mp'}, dimensions={0}, use_global_device_ids=true | all-gather | bytes 286720 | tf_op jit(solution)/shard_map/while/body/eval_jaxpr/all_gather | solution.py:134
  75.7 3.3 fusion.70
  79.2 1.2 concatenate.19
  81.8 85.1 %all-reduce.9.cloned.1.call-done = f32[128,2176]{1,0:T(8,128)} async-done(((f32[128,2176]{1,0:T(8,128)}), f32[128,2176]{1,0:T(8,128)}) %all-reduce.9.cloned.1.call-update) | async-done | bytes 1114128 | tf_op jit(solution)/shard_map/while
  167.7 1.3 collective-permute-start
  169.8 1.0 collective-permute-done
  171.7 23.1 %all_gather.20 = bf16[128,2048]{1,0:T(8,128)(2,1)S(1)} all-gather(bf16[8,2048]{1,0:T(8,128)(2,1)S(1)} %dynamic-slice_select_fusion.2), channel_id=1, replica_groups=mesh['section'=2,'dp'=16,'mp'=4] {'dp'}, dimensions={0}, use_global_device_ids=true | all-gather | bytes 557056 | tf_op jit(solution)/shard_map/while/body/eval_jaxpr/all_gather | solution.py:110
  194.8 1.2 fusion.66
  196.0 3.4 fusion.68
  199.4 1.6 fusion.67
  202.0 1.1 fusion.71
  203.0 19.2 %reduce-scatter.3.cloned.1.call-done = f32[32,1024]{1,0:T(8,128)} async-done(((f32[128,1024]{1,0:T(8,128)}), f32[32,1024]{1,0:T(8,128)}) %reduce-scatter.3.cloned.1.call-update) | async-done | bytes 131088 | tf_op jit(solution)/shard_map/while/body/eval_jaxpr/reduce_scatter | solution.py:116
  223.1 12.2 %all_gather.21 = bf16[128,896]{1,0:T(8,128)(2,1)S(1)} all-gather(bf16[32,896]{1,0:T(8,128)(2,1)S(1)} %fusion.69), channel_id=1, replica_groups=mesh['section'=2,'dp'=16,'mp'=4] {'mp'}, dimensions={0}, use_global_device_ids=true | all-gather | bytes 286720 | tf_op jit(solution)/shard_map/while/body/eval_jaxpr/all_gather | solution.py:134
  235.3 3.3 fusion.70
  238.9 1.2 concatenate.19
  241.4 85.1 %all-reduce.9.cloned.1.call-done = f32[128,2176]{1,0:T(8,128)} async-done(((f32[128,2176]{1,0:T(8,128)}), f32[128,2176]{1,0:T(8,128)}) %all-reduce.9.cloned.1.call-update) | async-done | bytes 1114128 | tf_op jit(solution)/shard_map/while
  327.4 1.3 collective-permute-start
  329.5 1.0 collective-permute-done
  331.3 23.1 %all_gather.20 = bf16[128,2048]{1,0:T(8,128)(2,1)S(1)} all-gather(bf16[8,2048]{1,0:T(8,128)(2,1)S(1)} %dynamic-slice_select_fusion.2), channel_id=1, replica_groups=mesh['section'=2,'dp'=16,'mp'=4] {'dp'}, dimensions={0}, use_global_device_ids=true | all-gather | bytes 557056 | tf_op jit(solution)/shard_map/while/body/eval_jaxpr/all_gather | solution.py:110
  354.5 1.2 fusion.66
  355.7 3.4 fusion.68
  359.1 1.6 fusion.67
  361.6 1.1 fusion.71
  362.7 19.2 %reduce-scatter.3.cloned.1.call-done = f32[32,1024]{1,0:T(8,128)} async-done(((f32[128,1024]{1,0:T(8,128)}), f32[32,1024]{1,0:T(8,128)}) %reduce-scatter.3.cloned.1.call-update) | async-done | bytes 131088 | tf_op jit(solution)/shard_map/while/body/eval_jaxpr/reduce_scatter | solution.py:116
  382.8 12.2 %all_gather.21 = bf16[128,896]{1,0:T(8,128)(2,1)S(1)} all-gather(bf16[32,896]{1,0:T(8,128)(2,1)S(1)} %fusion.69), channel_id=1, replica_groups=mesh['section'=2,'dp'=16,'mp'=4] {'mp'}, dimensions={0}, use_global_device_ids=true | all-gather | bytes 286720 | tf_op jit(solution)/shard_map/while/body/eval_jaxpr/all_gather | solution.py:134
  395.0 3.3 fusion.70
  398.6 1.2 concatenate.19
  401.1 85.1 %all-reduce.9.cloned.1.call-done = f32[128,2176]{1,0:T(8,128)} async-done(((f32[128,2176]{1,0:T(8,128)}), f32[128,2176]{1,0:T(8,128)}) %all-reduce.9.cloned.1.call-update) | async-done | bytes 1114128 | tf_op jit(solution)/shard_map/while
  487.1 1.3 collective-permute-start
  489.2 1.0 collective-permute-done
  491.0 23.1 %all_gather.20 = bf16[128,2048]{1,0:T(8,128)(2,1)S(1)} all-gather(bf16[8,2048]{1,0:T(8,128)(2,1)S(1)} %dynamic-slice_select_fusion.2), channel_id=1, replica_groups=mesh['section'=2,'dp'=16,'mp'=4] {'dp'}, dimensions={0}, use_global_device_ids=true | all-gather | bytes 557056 | tf_op jit(solution)/shard_map/while/body/eval_jaxpr/all_gather | solution.py:110
  514.1 1.2 fusion.66
  515.4 3.4 fusion.68
  518.8 1.6 fusion.67
  521.3 1.1 fusion.71
  522.4 19.2 %reduce-scatter.3.cloned.1.call-done = f32[32,1024]{1,0:T(8,128)} async-done(((f32[128,1024]{1,0:T(8,128)}), f32[32,1024]{1,0:T(8,128)}) %reduce-scatter.3.cloned.1.call-update) | async-done | bytes 131088 | tf_op jit(solution)/shard_map/while/body/eval_jaxpr/reduce_scatter | solution.py:116
  542.5 12.2 %all_gather.21 = bf16[128,896]{1,0:T(8,128)(2,1)S(1)} all-gather(bf16[32,896]{1,0:T(8,128)(2,1)S(1)} %fusion.69), channel_id=1, replica_groups=mesh['section'=2,'dp'=16,'mp'=4] {'mp'}, dimensions={0}, use_global_device_ids=true | all-gather | bytes 286720 | tf_op jit(solution)/shard_map/while/body/eval_jaxpr/all_gather | solution.py:134
  554.7 3.3 fusion.70
  558.2 1.2 concatenate.19
  560.8 85.1 %all-reduce.9.cloned.1.call-done = f32[128,2176]{1,0:T(8,128)} async-done(((f32[128,2176]{1,0:T(8,128)}), f32[128,2176]{1,0:T(8,128)}) %all-reduce.9.cloned.1.call-update) | async-done | bytes 1114128 | tf_op jit(solution)/shard_map/while
  646.8 1.3 collective-permute-start
  650.7 23.1 %all_gather.20 = bf16[128,2048]{1,0:T(8,128)(2,1)S(1)} all-gather(bf16[8,2048]{1,0:T(8,128)(2,1)S(1)} %dynamic-slice_select_fusion.2), channel_id=1, replica_groups=mesh['section'=2,'dp'=16,'mp'=4] {'dp'}, dimensions={0}, use_global_device_ids=true | all-gather | bytes 557056 | tf_op jit(solution)/shard_map/while/body/eval_jaxpr/all_gather | solution.py:110
  673.8 1.2 fusion.66
  675.1 3.4 fusion.68
  678.4 1.6 fusion.67
  681.0 1.1 fusion.71
  682.1 19.2 %reduce-scatter.3.cloned.1.call-done = f32[32,1024]{1,0:T(8,128)} async-done(((f32[128,1024]{1,0:T(8,128)}), f32[32,1024]{1,0:T(8,128)}) %reduce-scatter.3.cloned.1.call-update) | async-done | bytes 131088 | tf_op jit(solution)/shard_map/while/body/eval_jaxpr/reduce_scatter | solution.py:116
  702.1 12.2 %all_gather.21 = bf16[128,896]{1,0:T(8,128)(2,1)S(1)} all-gather(bf16[32,896]{1,0:T(8,128)(2,1)S(1)} %fusion.69), channel_id=1, replica_groups=mesh['section'=2,'dp'=16,'mp'=4] {'mp'}, dimensions={0}, use_global_device_ids=true | all-gather | bytes 286720 | tf_op jit(solution)/shard_map/while/body/eval_jaxpr/all_gather | solution.py:134
  714.3 3.3 fusion.70
  717.9 1.2 concatenate.19
  720.5 85.1 %all-reduce.9.cloned.1.call-done = f32[128,2176]{1,0:T(8,128)} async-done(((f32[128,2176]{1,0:T(8,128)}), f32[128,2176]{1,0:T(8,128)}) %all-reduce.9.cloned.1.call-update) | async-done | bytes 1114128 | tf_op jit(solution)/shard_map/while
  806.4 1.3 collective-permute-start
  811.0 1.9 convolution_bitcast_fusion
  812.9 1.9 convolution_bitcast_fusion.1
  814.8 3.8 pad_maximum_fusion.1
  820.5 166.7 %all-reduce.7.cloned.1.call-done = f32[2,256,4096]{2,1,0:T(8,128)} async-done(((f32[2,256,4096]{2,1,0:T(8,128)}), f32[2,256,4096]{2,1,0:T(8,128)}) %all-reduce.7.cloned.1.call-update) | async-done | bytes 8388624
  987.2 1.6 dynamic-slice_bitcast_fusion
  (147 shorter events, 30.9 us)
Async XLA Ops:
  8.1 802.5 %copy-start.4 = (s32[512]{0:T(512)S(1)}, s32[512]{0:T(512)}, u32[]{:S(2)}) copy-start(s32[512]{0:T(512)} %param.26) | copy-start | bytes 6148
  8.1 802.7 %copy-start.5 = (s32[256]{0:T(256)S(1)}, s32[256]{0:T(256)}, u32[]{:S(2)}) copy-start(s32[256]{0:T(256)} %param.27) | copy-start | bytes 3076
  8.1 29.9 %copy-start = (bf16[64,3584]{1,0:T(8,128)(2,1)S(1)}, bf16[64,3584]{1,0:T(8,128)(2,1)}, u32[]{:S(2)}) copy-start(bf16[64,3584]{1,0:T(8,128)(2,1)} %get-tuple-element.691) | copy-start | bytes 1376260 | tf_op jit(solution)/shard_map/while
  8.1 54.4 %reduce-scatter.3.cloned.1.call-start = ((), (), s32[]{:S(2)}) async-start(), calls=%async_computation.2 | async-start | bytes 655360 | tf_op jit(solution)/shard_map/while/body/eval_jaxpr/reduce_scatter | solution.py:116
  34.6 5.9 copy-start.2
  39.5 39.5 %copy-start.1 = (bf16[64,896]{1,0:T(8,128)(2,1)S(1)}, bf16[64,896]{1,0:T(8,128)(2,1)}, u32[]{:S(2)}) copy-start(bf16[64,896]{1,0:T(8,128)(2,1)} %get-tuple-element.697) | copy-start | bytes 344068 | tf_op jit(solution)/shard_map/while
  40.5 126.4 %all-reduce.9.cloned.1.call-start = ((), (), s32[]{:S(2)}) async-start(), calls=%async_computation.3 | async-start | bytes 2228224 | tf_op jit(solution)/shard_map/while
  75.7 4.8 copy-start.7
  75.7 6.1 slice-start
  167.7 3.1 collective-permute-start
  170.8 28.6 %copy-start = (bf16[64,3584]{1,0:T(8,128)(2,1)S(1)}, bf16[64,3584]{1,0:T(8,128)(2,1)}, u32[]{:S(2)}) copy-start(bf16[64,3584]{1,0:T(8,128)(2,1)} %get-tuple-element.691) | copy-start | bytes 1376260 | tf_op jit(solution)/shard_map/while
  170.8 51.4 %reduce-scatter.3.cloned.1.call-start = ((), (), s32[]{:S(2)}) async-start(), calls=%async_computation.2 | async-start | bytes 655360 | tf_op jit(solution)/shard_map/while/body/eval_jaxpr/reduce_scatter | solution.py:116
  196.0 5.9 copy-start.2
  201.0 37.7 %copy-start.1 = (bf16[64,896]{1,0:T(8,128)(2,1)S(1)}, bf16[64,896]{1,0:T(8,128)(2,1)}, u32[]{:S(2)}) copy-start(bf16[64,896]{1,0:T(8,128)(2,1)} %get-tuple-element.697) | copy-start | bytes 344068 | tf_op jit(solution)/shard_map/while
  201.9 124.6 %all-reduce.9.cloned.1.call-start = ((), (), s32[]{:S(2)}) async-start(), calls=%async_computation.3 | async-start | bytes 2228224 | tf_op jit(solution)/shard_map/while
  235.3 4.8 copy-start.7
  235.3 6.1 slice-start
  327.4 3.1 collective-permute-start
  330.5 28.6 %copy-start = (bf16[64,3584]{1,0:T(8,128)(2,1)S(1)}, bf16[64,3584]{1,0:T(8,128)(2,1)}, u32[]{:S(2)}) copy-start(bf16[64,3584]{1,0:T(8,128)(2,1)} %get-tuple-element.691) | copy-start | bytes 1376260 | tf_op jit(solution)/shard_map/while
  330.5 51.4 %reduce-scatter.3.cloned.1.call-start = ((), (), s32[]{:S(2)}) async-start(), calls=%async_computation.2 | async-start | bytes 655360 | tf_op jit(solution)/shard_map/while/body/eval_jaxpr/reduce_scatter | solution.py:116
  355.7 5.9 copy-start.2
  360.7 37.7 %copy-start.1 = (bf16[64,896]{1,0:T(8,128)(2,1)S(1)}, bf16[64,896]{1,0:T(8,128)(2,1)}, u32[]{:S(2)}) copy-start(bf16[64,896]{1,0:T(8,128)(2,1)} %get-tuple-element.697) | copy-start | bytes 344068 | tf_op jit(solution)/shard_map/while
  361.6 124.6 %all-reduce.9.cloned.1.call-start = ((), (), s32[]{:S(2)}) async-start(), calls=%async_computation.3 | async-start | bytes 2228224 | tf_op jit(solution)/shard_map/while
  395.0 4.8 copy-start.7
  395.0 6.1 slice-start
  487.1 3.1 collective-permute-start
  490.2 28.6 %copy-start = (bf16[64,3584]{1,0:T(8,128)(2,1)S(1)}, bf16[64,3584]{1,0:T(8,128)(2,1)}, u32[]{:S(2)}) copy-start(bf16[64,3584]{1,0:T(8,128)(2,1)} %get-tuple-element.691) | copy-start | bytes 1376260 | tf_op jit(solution)/shard_map/while
  490.2 51.4 %reduce-scatter.3.cloned.1.call-start = ((), (), s32[]{:S(2)}) async-start(), calls=%async_computation.2 | async-start | bytes 655360 | tf_op jit(solution)/shard_map/while/body/eval_jaxpr/reduce_scatter | solution.py:116
  515.4 5.9 copy-start.2
  520.3 37.7 %copy-start.1 = (bf16[64,896]{1,0:T(8,128)(2,1)S(1)}, bf16[64,896]{1,0:T(8,128)(2,1)}, u32[]{:S(2)}) copy-start(bf16[64,896]{1,0:T(8,128)(2,1)} %get-tuple-element.697) | copy-start | bytes 344068 | tf_op jit(solution)/shard_map/while
  521.2 124.6 %all-reduce.9.cloned.1.call-start = ((), (), s32[]{:S(2)}) async-start(), calls=%async_computation.3 | async-start | bytes 2228224 | tf_op jit(solution)/shard_map/while
  554.7 4.8 copy-start.7
  554.7 6.1 slice-start
  646.8 3.1 collective-permute-start
  649.9 28.6 %copy-start = (bf16[64,3584]{1,0:T(8,128)(2,1)S(1)}, bf16[64,3584]{1,0:T(8,128)(2,1)}, u32[]{:S(2)}) copy-start(bf16[64,3584]{1,0:T(8,128)(2,1)} %get-tuple-element.691) | copy-start | bytes 1376260 | tf_op jit(solution)/shard_map/while
  649.9 51.4 %reduce-scatter.3.cloned.1.call-start = ((), (), s32[]{:S(2)}) async-start(), calls=%async_computation.2 | async-start | bytes 655360 | tf_op jit(solution)/shard_map/while/body/eval_jaxpr/reduce_scatter | solution.py:116
  675.1 5.9 copy-start.2
  680.0 37.7 %copy-start.1 = (bf16[64,896]{1,0:T(8,128)(2,1)S(1)}, bf16[64,896]{1,0:T(8,128)(2,1)}, u32[]{:S(2)}) copy-start(bf16[64,896]{1,0:T(8,128)(2,1)} %get-tuple-element.697) | copy-start | bytes 344068 | tf_op jit(solution)/shard_map/while
  680.9 124.6 %all-reduce.9.cloned.1.call-start = ((), (), s32[]{:S(2)}) async-start(), calls=%async_computation.3 | async-start | bytes 2228224 | tf_op jit(solution)/shard_map/while
  714.3 4.8 copy-start.7
  714.3 6.1 slice-start
  806.4 3.1 collective-permute-start
  809.5 5.3 copy-start.3
  809.5 177.7 %all-reduce.7.cloned.1.call-start = ((), (), s32[]{:S(2)}) async-start(), calls=%async_computation.1 | async-start | bytes 16777216
  818.6 0.7 copy-start.6
Sparse Core Ops, SparseCore 0:
  40.6 21.9 reduce-scatter.2
  80.6 86.2 all-reduce.8
  202.0 20.1 reduce-scatter.2
  240.3 86.2 all-reduce.8
  361.7 20.1 reduce-scatter.2
  399.9 86.2 all-reduce.8
  521.4 20.1 reduce-scatter.2
  559.6 86.2 all-reduce.8
  681.0 20.1 reduce-scatter.2
  719.3 86.2 all-reduce.8
Sparse Core Ops, SparseCore 1:
  818.7 168.4 all-reduce.6
where the time goes:
time: 998 us; the launch traced here: 996 us
  waiting for transfers between devices  695 us (70%)
  blocking collectives  178 us (18%)
  matrix products  57.8 us (6%)
  other arithmetic  22.3 us (2%)
  local copies, waits for them, and re-layouts  16.5 us (2%)
  between operations  16.2 us (2%)
    while x15, waiting for transfers between devices  426 us
    unnamed x2, waiting for transfers between devices  167 us
    all_gather x5, blocking collectives, advance(): gathered_up = lax.all_gather(grad_up, 'dp', axis=0, tiled=True)  117 us
    reduce_scatter x5, waiting for transfers between devices, advance(): lax.psum_scatter(jnp.concatenate([times_t(grad_rows, weight_up), times_t(...  97.6 us
    all_gather x5, blocking collectives, advance(): gathered_low = lax.all_gather(grad_mid, 'mp', axis=0, tiled=True)  61 us
    dot_general x30, matrix products, times_t(): lax.dot_general(left, right, (((1,), (1,)), ((), ())), preferred_element_...  54 us
  transfers between devices with their start and end apart: 16, of which 16 were waited for; matrix products, arithmetic and copies ran while one was open for 1% of the time, Pallas kernels for 0%

commit v1 on v0

--- a/solution.py
+++ b/solution.py
@@ -2,6 +2,11 @@
 import jax.numpy as jnp
 from jax import lax
 from jax.sharding import PartitionSpec as P
+
+
+def views_place(block_in):
+    e_now = lax.all_to_all(jnp.stack([block_in] * lax.psum(1, "dp"), axis=0), "dp", 0, 0)
+    return jnp.concatenate(e_now, axis=0)
 
 
 def from_behind(block, axis, distance):
@@ -107,7 +112,7 @@
         first_row = block_safe * rows_block
         top_block = lax.dynamic_slice_in_dim(out_grad, first_row, rows_block, 0)
         grad_up = jnp.where(section_index == section_count - 1, top_block, received)
-        gathered_up = lax.all_gather(grad_up, "dp", axis=0, tiled=True)
+        gathered_up = views_place(grad_up)
         inputs_up = lax.dynamic_slice_in_dim(acts_upper, first_row, rows_block, 1).reshape(
             dp_count * rows_block, width_hidden
         )

time: 998 us -> 957 us (0.959)
  blocking collectives: 178 us -> 61 us
  waiting for transfers between devices: 695 us -> 740 us
  starting transfers between devices: 6.73 us -> 33 us
    all_gather x5 -> x0, blocking collectives: 117 us -> none  [advance(): gathered_up = lax.all_gather(grad_up, 'dp', axis=0, tiled=True)]
    all_to_all x0 -> x5, waiting for transfers between devices: none -> 50.3 us  [views_place(): lax.all_to_all(jnp.stack([block_in] * lax.psum(1, 'dp'), axis=0), 'dp', 0...]
    all_to_all x0 -> x5, starting transfers between devices: none -> 26.1 us  [views_place(): lax.all_to_all(jnp.stack([block_in] * lax.psum(1, 'dp'), axis=0), 'dp', 0...]
  transfers between devices with their start and end apart: 16 -> 21, of which waited for: 16 -> 21; matrix products, arithmetic and copies ran while one was open for 1% -> 2% of each run, Pallas kernels for 0% -> 0%
where the time goes in v1:
time: 957 us; the launch traced here: 955 us
  waiting for transfers between devices  740 us (77%)
  blocking collectives  61 us (6%)
  matrix products  58.2 us (6%)
  starting transfers between devices  33 us (3%)
  other arithmetic  22 us (2%)
  local copies, waits for them, and re-layouts  20.5 us (2%)
  between operations  16.2 us (2%)
    while x15, waiting for transfers between devices  426 us
    unnamed x2, waiting for transfers between devices  167 us
    reduce_scatter x5, waiting for transfers between devices, advance(): lax.psum_scatter(jnp.concatenate([times_t(grad_rows, weight_up), times_t(...  92.1 us
    all_gather x5, blocking collectives, advance(): gathered_low = lax.all_gather(grad_mid, 'mp', axis=0, tiled=True)  61 us
    dot_general x30, matrix products, times_t(): lax.dot_general(left, right, (((1,), (1,)), ((), ())), preferred_element_...  54.4 us
    all_to_all x5, waiting for transfers between devices, views_place(): lax.all_to_all(jnp.stack([block_in] * lax.psum(1, 'dp'), axis=0), 'dp', 0...  50.3 us
    all_to_all x5, starting transfers between devices, views_place(): lax.all_to_all(jnp.stack([block_in] * lax.psum(1, 'dp'), axis=0), 'dp', 0...  26.1 us
  transfers between devices with their start and end apart: 21, of which 21 were waited for; matrix products, arithmetic and copies ran while one was open for 2% of the time, Pallas kernels for 0%

profile of v1, /device:TPU:0, one launch (start us, length us, event | category | flops | bytes accessed | tf_op | source)
XLA Modules:
  0.0 955.1 jit_solution(31331529685006422)
XLA Ops:
  8.1 760.0 %while.21 = (s32[]{:T(128)}, bf16[8,2048]{1,0:T(8,128)(2,1)S(1)}, bf16[32,2048]{1,0:T(8,128)(2,1)S(1)}, f32[4,2,128]{2,1,0:T(2,128)S(1)}, f32[4,2,128]{2,1,0:T(2...) while((s32[]{:T(128)}, bf16[8,2048]{1,0:T(8,128)(2,1)S(1)}, ...), condition=%wide.region_3.4_spmd, body=%wide.region_0.3_spmd.sunk | while | flops 1055576576 | bytes 28222164 | solution.py:182
  9.7 7.1 all-to-all-start
  16.9 1.7 fusion.67
  18.6 9.8 %all-to-all-done = bf16[16,8,2048]{2,1,0:T(8,128)(2,1)S(1)} async-done(((bf16[16,8,2048]{2,1,0:T(8,128)(2,1)}), bf16[16,8,2048]{2,1,0:T(8,128)(2,1)S(1)}, u32[]{:S(2)}, u32[]{:S(2)}) %all-to-all-start) | async-done | bytes 524320 | tf_op jit(solution)/shard_map/while/body/eval_jaxpr/all_to_all | solution.py:8
  28.4 1.2 fusion.66
  29.6 3.3 fusion.68
  34.0 1.1 fusion.71
  35.0 19.1 %reduce-scatter.3.cloned.1.call-done = f32[32,1024]{1,0:T(8,128)} async-done(((f32[128,1024]{1,0:T(8,128)}), f32[32,1024]{1,0:T(8,128)}) %reduce-scatter.3.cloned.1.call-update) | async-done | bytes 131088 | tf_op jit(solution)/shard_map/while/body/eval_jaxpr/reduce_scatter | solution.py:121
  55.1 12.2 %all_gather.10 = bf16[128,896]{1,0:T(8,128)(2,1)S(1)} all-gather(bf16[32,896]{1,0:T(8,128)(2,1)S(1)} %fusion.69), channel_id=1, replica_groups=mesh['section'=2,'dp'=16,'mp'=4] {'mp'}, dimensions={0}, use_global_device_ids=true | all-gather | bytes 286720 | tf_op jit(solution)/shard_map/while/body/eval_jaxpr/all_gather | solution.py:139
  67.3 3.3 fusion.70
  70.9 1.2 concatenate.19
  73.4 85.1 %all-reduce.9.cloned.1.call-done = f32[128,2176]{1,0:T(8,128)} async-done(((f32[128,2176]{1,0:T(8,128)}), f32[128,2176]{1,0:T(8,128)}) %all-reduce.9.cloned.1.call-update) | async-done | bytes 1114128 | tf_op jit(solution)/shard_map/while
  159.3 1.3 collective-permute-start
  164.0 4.8 all-to-all-start
  168.9 1.7 fusion.67
  170.6 10.1 %all-to-all-done = bf16[16,8,2048]{2,1,0:T(8,128)(2,1)S(1)} async-done(((bf16[16,8,2048]{2,1,0:T(8,128)(2,1)}), bf16[16,8,2048]{2,1,0:T(8,128)(2,1)S(1)}, u32[]{:S(2)}, u32[]{:S(2)}) %all-to-all-start) | async-done | bytes 524320 | tf_op jit(solution)/shard_map/while/body/eval_jaxpr/all_to_all | solution.py:8
  180.7 1.2 fusion.66
  181.9 3.3 fusion.68
  186.2 1.1 fusion.71
  187.3 18.3 %reduce-scatter.3.cloned.1.call-done = f32[32,1024]{1,0:T(8,128)} async-done(((f32[128,1024]{1,0:T(8,128)}), f32[32,1024]{1,0:T(8,128)}) %reduce-scatter.3.cloned.1.call-update) | async-done | bytes 131088 | tf_op jit(solution)/shard_map/while/body/eval_jaxpr/reduce_scatter | solution.py:121
  206.5 12.2 %all_gather.10 = bf16[128,896]{1,0:T(8,128)(2,1)S(1)} all-gather(bf16[32,896]{1,0:T(8,128)(2,1)S(1)} %fusion.69), channel_id=1, replica_groups=mesh['section'=2,'dp'=16,'mp'=4] {'mp'}, dimensions={0}, use_global_device_ids=true | all-gather | bytes 286720 | tf_op jit(solution)/shard_map/while/body/eval_jaxpr/all_gather | solution.py:139
  218.7 3.3 fusion.70
  222.3 1.2 concatenate.19
  224.8 85.1 %all-reduce.9.cloned.1.call-done = f32[128,2176]{1,0:T(8,128)} async-done(((f32[128,2176]{1,0:T(8,128)}), f32[128,2176]{1,0:T(8,128)}) %all-reduce.9.cloned.1.call-update) | async-done | bytes 1114128 | tf_op jit(solution)/shard_map/while
  310.7 1.3 collective-permute-start
  315.5 4.8 all-to-all-start
  320.3 1.7 fusion.67
  322.0 10.1 %all-to-all-done = bf16[16,8,2048]{2,1,0:T(8,128)(2,1)S(1)} async-done(((bf16[16,8,2048]{2,1,0:T(8,128)(2,1)}), bf16[16,8,2048]{2,1,0:T(8,128)(2,1)S(1)}, u32[]{:S(2)}, u32[]{:S(2)}) %all-to-all-start) | async-done | bytes 524320 | tf_op jit(solution)/shard_map/while/body/eval_jaxpr/all_to_all | solution.py:8
  332.1 1.2 fusion.66
  333.3 3.3 fusion.68
  337.6 1.1 fusion.71
  338.7 18.2 %reduce-scatter.3.cloned.1.call-done = f32[32,1024]{1,0:T(8,128)} async-done(((f32[128,1024]{1,0:T(8,128)}), f32[32,1024]{1,0:T(8,128)}) %reduce-scatter.3.cloned.1.call-update) | async-done | bytes 131088 | tf_op jit(solution)/shard_map/while/body/eval_jaxpr/reduce_scatter | solution.py:121
  357.9 12.2 %all_gather.10 = bf16[128,896]{1,0:T(8,128)(2,1)S(1)} all-gather(bf16[32,896]{1,0:T(8,128)(2,1)S(1)} %fusion.69), channel_id=1, replica_groups=mesh['section'=2,'dp'=16,'mp'=4] {'mp'}, dimensions={0}, use_global_device_ids=true | all-gather | bytes 286720 | tf_op jit(solution)/shard_map/while/body/eval_jaxpr/all_gather | solution.py:139
  370.1 3.3 fusion.70
  373.7 1.2 concatenate.19
  376.2 85.1 %all-reduce.9.cloned.1.call-done = f32[128,2176]{1,0:T(8,128)} async-done(((f32[128,2176]{1,0:T(8,128)}), f32[128,2176]{1,0:T(8,128)}) %all-reduce.9.cloned.1.call-update) | async-done | bytes 1114128 | tf_op jit(solution)/shard_map/while
  462.2 1.3 collective-permute-start
  466.9 4.8 all-to-all-start
  471.7 1.7 fusion.67
  473.4 10.1 %all-to-all-done = bf16[16,8,2048]{2,1,0:T(8,128)(2,1)S(1)} async-done(((bf16[16,8,2048]{2,1,0:T(8,128)(2,1)}), bf16[16,8,2048]{2,1,0:T(8,128)(2,1)S(1)}, u32[]{:S(2)}, u32[]{:S(2)}) %all-to-all-start) | async-done | bytes 524320 | tf_op jit(solution)/shard_map/while/body/eval_jaxpr/all_to_all | solution.py:8
  483.5 1.2 fusion.66
  484.7 3.3 fusion.68
  490.1 18.2 %reduce-scatter.3.cloned.1.call-done = f32[32,1024]{1,0:T(8,128)} async-done(((f32[128,1024]{1,0:T(8,128)}), f32[32,1024]{1,0:T(8,128)}) %reduce-scatter.3.cloned.1.call-update) | async-done | bytes 131088 | tf_op jit(solution)/shard_map/while/body/eval_jaxpr/reduce_scatter | solution.py:121
  509.3 12.2 %all_gather.10 = bf16[128,896]{1,0:T(8,128)(2,1)S(1)} all-gather(bf16[32,896]{1,0:T(8,128)(2,1)S(1)} %fusion.69), channel_id=1, replica_groups=mesh['section'=2,'dp'=16,'mp'=4] {'mp'}, dimensions={0}, use_global_device_ids=true | all-gather | bytes 286720 | tf_op jit(solution)/shard_map/while/body/eval_jaxpr/all_gather | solution.py:139
  521.5 3.3 fusion.70
  525.1 1.2 concatenate.19
  527.6 85.1 %all-reduce.9.cloned.1.call-done = f32[128,2176]{1,0:T(8,128)} async-done(((f32[128,2176]{1,0:T(8,128)}), f32[128,2176]{1,0:T(8,128)}) %all-reduce.9.cloned.1.call-update) | async-done | bytes 1114128 | tf_op jit(solution)/shard_map/while
  613.6 1.3 collective-permute-start
  618.3 4.8 all-to-all-start
  623.1 1.7 fusion.67
  624.8 10.1 %all-to-all-done = bf16[16,8,2048]{2,1,0:T(8,128)(2,1)S(1)} async-done(((bf16[16,8,2048]{2,1,0:T(8,128)(2,1)}), bf16[16,8,2048]{2,1,0:T(8,128)(2,1)S(1)}, u32[]{:S(2)}, u32[]{:S(2)}) %all-to-all-start) | async-done | bytes 524320 | tf_op jit(solution)/shard_map/while/body/eval_jaxpr/all_to_all | solution.py:8
  634.9 1.2 fusion.66
  636.2 3.3 fusion.68
  641.6 18.2 %reduce-scatter.3.cloned.1.call-done = f32[32,1024]{1,0:T(8,128)} async-done(((f32[128,1024]{1,0:T(8,128)}), f32[32,1024]{1,0:T(8,128)}) %reduce-scatter.3.cloned.1.call-update) | async-done | bytes 131088 | tf_op jit(solution)/shard_map/while/body/eval_jaxpr/reduce_scatter | solution.py:121
  660.7 12.2 %all_gather.10 = bf16[128,896]{1,0:T(8,128)(2,1)S(1)} all-gather(bf16[32,896]{1,0:T(8,128)(2,1)S(1)} %fusion.69), channel_id=1, replica_groups=mesh['section'=2,'dp'=16,'mp'=4] {'mp'}, dimensions={0}, use_global_device_ids=true | all-gather | bytes 286720 | tf_op jit(solution)/shard_map/while/body/eval_jaxpr/all_gather | solution.py:139
  672.9 3.3 fusion.70
  676.5 1.2 concatenate.19
  679.0 85.1 %all-reduce.9.cloned.1.call-done = f32[128,2176]{1,0:T(8,128)} async-done(((f32[128,2176]{1,0:T(8,128)}), f32[128,2176]{1,0:T(8,128)}) %all-reduce.9.cloned.1.call-update) | async-done | bytes 1114128 | tf_op jit(solution)/shard_map/while
  765.0 1.3 collective-permute-start
  769.6 1.9 convolution_bitcast_fusion
  771.5 1.9 convolution_bitcast_fusion.1
  773.4 3.8 pad_maximum_fusion.1
  779.1 167.0 %all-reduce.7.cloned.1.call-done = f32[2,256,4096]{2,1,0:T(8,128)} async-done(((f32[2,256,4096]{2,1,0:T(8,128)}), f32[2,256,4096]{2,1,0:T(8,128)}) %all-reduce.7.cloned.1.call-update) | async-done | bytes 8388624
  946.0 1.6 dynamic-slice_bitcast_fusion
  (147 shorter events, 40.2 us)
Async XLA Ops:
  8.1 761.0 %copy-start.3 = (s32[512]{0:T(512)S(1)}, s32[512]{0:T(512)}, u32[]{:S(2)}) copy-start(s32[512]{0:T(512)} %param.26) | copy-start | bytes 6148
  8.1 761.3 %copy-start.4 = (s32[256]{0:T(256)S(1)}, s32[256]{0:T(256)}, u32[]{:S(2)}) copy-start(s32[256]{0:T(256)} %param.27) | copy-start | bytes 3076
  9.7 18.7 %all-to-all-start = ((bf16[16,8,2048]{2,1,0:T(8,128)(2,1)}), bf16[16,8,2048]{2,1,0:T(8,128)(2,1)S(1)}, u32[]{:S(2)}, u32[]{:S(2)}) async-start(bf16[16,8,2048]{2,1,0:T(8,128)(2,1)} %stack.16), calls=%async_computation | async-start | bytes 1048576 | tf_op jit(solution)/shard_map/while/body/eval_jaxpr/all_to_all | solution.py:8
  16.9 37.3 %reduce-scatter.3.cloned.1.call-start = ((), (), s32[]{:S(2)}) async-start(), calls=%async_computation.3 | async-start | bytes 655360 | tf_op jit(solution)/shard_map/while/body/eval_jaxpr/reduce_scatter | solution.py:121
  18.6 15.3 %copy-start.1 = (bf16[64,512]{1,0:T(8,128)(2,1)S(1)}, bf16[64,512]{1,0:T(8,128)(2,1)}, u32[]{:S(2)}) copy-start(bf16[64,512]{1,0:T(8,128)(2,1)} %get-tuple-element.696) | copy-start | bytes 196612 | tf_op jit(solution)/shard_map/while
  33.0 37.7 %copy-start = (bf16[64,896]{1,0:T(8,128)(2,1)S(1)}, bf16[64,896]{1,0:T(8,128)(2,1)}, u32[]{:S(2)}) copy-start(bf16[64,896]{1,0:T(8,128)(2,1)} %get-tuple-element.697) | copy-start | bytes 344068 | tf_op jit(solution)/shard_map/while
  33.9 124.6 %all-reduce.9.cloned.1.call-start = ((), (), s32[]{:S(2)}) async-start(), calls=%async_computation.4 | async-start | bytes 2228224 | tf_op jit(solution)/shard_map/while
  67.3 4.8 copy-start.6
  67.3 6.1 slice-start
  159.3 3.1 collective-permute-start
  164.0 16.6 %all-to-all-start = ((bf16[16,8,2048]{2,1,0:T(8,128)(2,1)}), bf16[16,8,2048]{2,1,0:T(8,128)(2,1)S(1)}, u32[]{:S(2)}, u32[]{:S(2)}) async-start(bf16[16,8,2048]{2,1,0:T(8,128)(2,1)} %stack.16), calls=%async_computation | async-start | bytes 1048576 | tf_op jit(solution)/shard_map/while/body/eval_jaxpr/all_to_all | solution.py:8
  168.8 36.8 %reduce-scatter.3.cloned.1.call-start = ((), (), s32[]{:S(2)}) async-start(), calls=%async_computation.3 | async-start | bytes 655360 | tf_op jit(solution)/shard_map/while/body/eval_jaxpr/reduce_scatter | solution.py:121
  170.5 15.7 %copy-start.1 = (bf16[64,512]{1,0:T(8,128)(2,1)S(1)}, bf16[64,512]{1,0:T(8,128)(2,1)}, u32[]{:S(2)}) copy-start(bf16[64,512]{1,0:T(8,128)(2,1)} %get-tuple-element.696) | copy-start | bytes 196612 | tf_op jit(solution)/shard_map/while
  185.2 36.8 %copy-start = (bf16[64,896]{1,0:T(8,128)(2,1)S(1)}, bf16[64,896]{1,0:T(8,128)(2,1)}, u32[]{:S(2)}) copy-start(bf16[64,896]{1,0:T(8,128)(2,1)} %get-tuple-element.697) | copy-start | bytes 344068 | tf_op jit(solution)/shard_map/while
  186.2 123.7 %all-reduce.9.cloned.1.call-start = ((), (), s32[]{:S(2)}) async-start(), calls=%async_computation.4 | async-start | bytes 2228224 | tf_op jit(solution)/shard_map/while
  218.7 4.8 copy-start.6
  218.7 6.1 slice-start
  310.7 3.1 collective-permute-start
  315.5 16.6 %all-to-all-start = ((bf16[16,8,2048]{2,1,0:T(8,128)(2,1)}), bf16[16,8,2048]{2,1,0:T(8,128)(2,1)S(1)}, u32[]{:S(2)}, u32[]{:S(2)}) async-start(bf16[16,8,2048]{2,1,0:T(8,128)(2,1)} %stack.16), calls=%async_computation | async-start | bytes 1048576 | tf_op jit(solution)/shard_map/while/body/eval_jaxpr/all_to_all | solution.py:8
  320.2 36.7 %reduce-scatter.3.cloned.1.call-start = ((), (), s32[]{:S(2)}) async-start(), calls=%async_computation.3 | async-start | bytes 655360 | tf_op jit(solution)/shard_map/while/body/eval_jaxpr/reduce_scatter | solution.py:121
  322.0 15.7 %copy-start.1 = (bf16[64,512]{1,0:T(8,128)(2,1)S(1)}, bf16[64,512]{1,0:T(8,128)(2,1)}, u32[]{:S(2)}) copy-start(bf16[64,512]{1,0:T(8,128)(2,1)} %get-tuple-element.696) | copy-start | bytes 196612 | tf_op jit(solution)/shard_map/while
  336.7 36.8 %copy-start = (bf16[64,896]{1,0:T(8,128)(2,1)S(1)}, bf16[64,896]{1,0:T(8,128)(2,1)}, u32[]{:S(2)}) copy-start(bf16[64,896]{1,0:T(8,128)(2,1)} %get-tuple-element.697) | copy-start | bytes 344068 | tf_op jit(solution)/shard_map/while
  337.6 123.7 %all-reduce.9.cloned.1.call-start = ((), (), s32[]{:S(2)}) async-start(), calls=%async_computation.4 | async-start | bytes 2228224 | tf_op jit(solution)/shard_map/while
  370.1 4.8 copy-start.6
  370.1 6.1 slice-start
  462.2 3.1 collective-permute-start
  466.9 16.6 %all-to-all-start = ((bf16[16,8,2048]{2,1,0:T(8,128)(2,1)}), bf16[16,8,2048]{2,1,0:T(8,128)(2,1)S(1)}, u32[]{:S(2)}, u32[]{:S(2)}) async-start(bf16[16,8,2048]{2,1,0:T(8,128)(2,1)} %stack.16), calls=%async_computation | async-start | bytes 1048576 | tf_op jit(solution)/shard_map/while/body/eval_jaxpr/all_to_all | solution.py:8
  471.6 36.7 %reduce-scatter.3.cloned.1.call-start = ((), (), s32[]{:S(2)}) async-start(), calls=%async_computation.3 | async-start | bytes 655360 | tf_op jit(solution)/shard_map/while/body/eval_jaxpr/reduce_scatter | solution.py:121
  473.4 15.7 %copy-start.1 = (bf16[64,512]{1,0:T(8,128)(2,1)S(1)}, bf16[64,512]{1,0:T(8,128)(2,1)}, u32[]{:S(2)}) copy-start(bf16[64,512]{1,0:T(8,128)(2,1)} %get-tuple-element.696) | copy-start | bytes 196612 | tf_op jit(solution)/shard_map/while
  488.1 36.8 %copy-start = (bf16[64,896]{1,0:T(8,128)(2,1)S(1)}, bf16[64,896]{1,0:T(8,128)(2,1)}, u32[]{:S(2)}) copy-start(bf16[64,896]{1,0:T(8,128)(2,1)} %get-tuple-element.697) | copy-start | bytes 344068 | tf_op jit(solution)/shard_map/while
  489.0 123.7 %all-reduce.9.cloned.1.call-start = ((), (), s32[]{:S(2)}) async-start(), calls=%async_computation.4 | async-start | bytes 2228224 | tf_op jit(solution)/shard_map/while
  521.5 4.8 copy-start.6
  521.5 6.1 slice-start
  613.6 3.1 collective-permute-start
  618.3 16.6 %all-to-all-start = ((bf16[16,8,2048]{2,1,0:T(8,128)(2,1)}), bf16[16,8,2048]{2,1,0:T(8,128)(2,1)S(1)}, u32[]{:S(2)}, u32[]{:S(2)}) async-start(bf16[16,8,2048]{2,1,0:T(8,128)(2,1)} %stack.16), calls=%async_computation | async-start | bytes 1048576 | tf_op jit(solution)/shard_map/while/body/eval_jaxpr/all_to_all | solution.py:8
  623.1 36.7 %reduce-scatter.3.cloned.1.call-start = ((), (), s32[]{:S(2)}) async-start(), calls=%async_computation.3 | async-start | bytes 655360 | tf_op jit(solution)/shard_map/while/body/eval_jaxpr/reduce_scatter | solution.py:121
  624.8 15.7 %copy-start.1 = (bf16[64,512]{1,0:T(8,128)(2,1)S(1)}, bf16[64,512]{1,0:T(8,128)(2,1)}, u32[]{:S(2)}) copy-start(bf16[64,512]{1,0:T(8,128)(2,1)} %get-tuple-element.696) | copy-start | bytes 196612 | tf_op jit(solution)/shard_map/while
  639.5 36.8 %copy-start = (bf16[64,896]{1,0:T(8,128)(2,1)S(1)}, bf16[64,896]{1,0:T(8,128)(2,1)}, u32[]{:S(2)}) copy-start(bf16[64,896]{1,0:T(8,128)(2,1)} %get-tuple-element.697) | copy-start | bytes 344068 | tf_op jit(solution)/shard_map/while
  640.4 123.7 %all-reduce.9.cloned.1.call-start = ((), (), s32[]{:S(2)}) async-start(), calls=%async_computation.4 | async-start | bytes 2228224 | tf_op jit(solution)/shard_map/while
  672.9 4.8 copy-start.6
  672.9 6.1 slice-start
  765.0 3.1 collective-permute-start
  768.1 5.3 copy-start.2
  768.1 177.9 %all-reduce.7.cloned.1.call-start = ((), (), s32[]{:S(2)}) async-start(), calls=%async_computation.2 | async-start | bytes 16777216
  777.2 0.7 copy-start.5
Sparse Core Ops, SparseCore 0:
  34.0 20.1 reduce-scatter.2
  72.2 86.1 all-reduce.8
  186.3 19.2 reduce-scatter.2
  223.6 86.2 all-reduce.8
  337.7 19.2 reduce-scatter.2
  375.0 86.2 all-reduce.8
  489.1 19.2 reduce-scatter.2
  526.4 86.2 all-reduce.8
  640.5 19.2 reduce-scatter.2
  677.8 86.2 all-reduce.8
Sparse Core Ops, SparseCore 1:
  777.3 168.7 all-reduce.6
